TPU v7x, 128 devices: a whole 4x4x4 slice. The times are simulated.
128 devices in a mesh: ctx: 64 (over z, x_hi, y, core), head: 2 (over x_lo).
Axes of the slice: x: 4 (x_hi: 2, x_lo: 2; x = x_hi * 2 + x_lo), y: 4, z: 4, core: 2. Of those that a mesh axis runs over, the one named last changes fastest.
Arguments:
- queries: bfloat16 [64, 1024, 2048], P('ctx', None, 'head'), may hold values from -8 to 8
- keys: bfloat16 [64, 1024, 2048], P('ctx', None, 'head'), may hold values from -8 to 8
- values: bfloat16 [64, 1024, 2048], P('ctx', None, 'head'), may hold values from -24 to 24
- w_out: bfloat16 [2048, 4096], P('head'), may hold values from -0.125 to 0.125
Outputs:
- mixed: bfloat16 [64, 1024, 4096], P('ctx', 'head')
All inputs are finite; a program needn't handle non-finite values.
Results may differ from a plain program's by a relative error of at most 0.013.
Values may be sent and summed in bfloat16 or wider, within the bound.
No kernel may reach another device: no remote copies, remote signals or barrier semaphores. Data moves between devices by JAX's collectives and lax.ppermute only.
A program may use at most 128 MiB of HBM per device.

v0:
```python
import jax
import jax.numpy as jnp
from jax import lax
from jax.sharding import PartitionSpec as P

HD = 128
GROUP = 4
masked_score = -1e30


def in_blocks(x, dim, devices):
    before, after = (x.shape[:dim], x.shape[dim + 1 :])
    return jnp.moveaxis(x.reshape(*before, devices, -1, *after), dim, 0)


def summed_on_arrival(x, axis, dim):
    devices = lax.axis_size(axis)
    parts = lax.all_to_all(in_blocks(x, dim, devices), axis, 0, 0, tiled=True)
    return jnp.sum(parts.astype(jnp.float32), axis=0)


def split_kinds(tensor, parity):
    groups = tensor.shape[2] // (2 * GROUP * HD)
    shaped = tensor.reshape((tensor.shape[0], tensor.shape[1], groups, 2, GROUP, HD))
    return shaped[:, :, :, parity].reshape((tensor.shape[0], tensor.shape[1], groups * GROUP, HD))


def normalized(scores):
    top = jnp.max(scores, axis=-1, keepdims=True)
    expo = jnp.exp(scores - top)
    total = jnp.sum(expo, axis=-1, keepdims=True)
    return (expo / total).astype(jnp.bfloat16)


def row_attention(queries, keys, values):
    scale = jnp.float32(1.0 / HD**0.5)
    length = queries.shape[1]
    causal = lax.broadcasted_iota(jnp.int32, (length, length), 1) <= lax.broadcasted_iota(
        jnp.int32, (length, length), 0
    )

    def one_row(triple):
        query_row, key_row, value_row = triple
        scores = (
            jnp.einsum("qhd,khd->hqk", query_row, key_row, preferred_element_type=jnp.float32)
            * scale
        )
        scores = jnp.where(causal, scores, masked_score)
        weights = normalized(scores)
        return jnp.einsum(
            "hqk,khd->qhd", weights, value_row, preferred_element_type=jnp.float32
        ).astype(jnp.bfloat16)

    return lax.map(one_row, (queries, keys, values))


def column_attention(triple):
    queries, keys, values = triple
    scale = jnp.float32(1.0 / HD**0.5)
    height = queries.shape[0]
    causal = lax.broadcasted_iota(jnp.int32, (height, height), 1) <= lax.broadcasted_iota(
        jnp.int32, (height, height), 0
    )
    scores = (
        jnp.einsum("rchd,schd->chrs", queries, keys, preferred_element_type=jnp.float32) * scale
    )
    scores = jnp.where(causal, scores, masked_score)
    weights = normalized(scores)
    attended = jnp.einsum(
        "chrs,schd->rchd", weights, values, preferred_element_type=jnp.float32
    ).astype(jnp.bfloat16)
    return lax.all_to_all(attended, "ctx", split_axis=0, concat_axis=1, tiled=True)


def on_device(queries, keys, values, w_out):
    rows_dev, stride, local_feat = queries.shape
    model_width = w_out.shape[1]
    groups = local_feat // (2 * GROUP * HD)
    row_out = row_attention(split_kinds(queries, 0), split_kinds(keys, 0), split_kinds(values, 0))
    col_triple = (split_kinds(queries, 1), split_kinds(keys, 1), split_kinds(values, 1))
    col_out = column_attention(
        (
            lax.all_to_all(col_triple[0], "ctx", split_axis=1, concat_axis=0, tiled=True),
            lax.all_to_all(col_triple[1], "ctx", split_axis=1, concat_axis=0, tiled=True),
            lax.all_to_all(col_triple[2], "ctx", split_axis=1, concat_axis=0, tiled=True),
        )
    )
    joined = jnp.stack(
        [
            row_out.reshape((rows_dev, stride, groups, GROUP, HD)),
            col_out.reshape((rows_dev, stride, groups, GROUP, HD)),
        ],
        axis=3,
    ).reshape((rows_dev * stride, local_feat))
    partial_value = jnp.dot(joined, w_out, preferred_element_type=jnp.float32)
    partial_value = partial_value.reshape((rows_dev, stride, model_width))
    return summed_on_arrival(partial_value.astype(jnp.bfloat16), "head", 1).astype(jnp.bfloat16)


def solution(mesh):
    return jax.shard_map(
        on_device,
        mesh=mesh,
        in_specs=(
            P("ctx", None, "head"),
            P("ctx", None, "head"),
            P("ctx", None, "head"),
            P("head", None),
        ),
        out_specs=P("ctx", "head", None),
        check_vma=False,
    )
```

profile of v0, /device:TPU:1, one launch (start us, length us, event | category | flops | bytes accessed | tf_op | source)
XLA Modules:
  0.0 234.4 jit_solution(8424355942385947717)
XLA Ops:
  0.0 2.9 %copy.40 = bf16[1,1024,1024]{1,2,0:T(8,128)(2,1)S(1)} copy(bf16[1,1024,1024]{2,1,0:T(8,128)(2,1)} %param.5) | data formatting | bytes 4194304 | tf_op args[1]
  2.9 0.0 copy-start
  2.9 0.1 slice_bitcast_fusion.1
  3.0 1.7 copy.46
  4.7 0.0 copy-done
  4.7 12.7 %all-to-all-start.1 = ((bf16[1,1024,4,128]{3,2,0,1:T(4,128)(2,1)}), bf16[1,1024,4,128]{3,2,0,1:T(4,128)(2,1)}, u32[]{:S(2)}, u32[]{:S(2)}) async-start(bf16[1,1024,4,128]{3,2,0,1:T(4,128)(2,1)} %copy.46), calls=%async_computation.1 | async-start | bytes 2097152 | tf_op jit(solution)/shard_map/all_to_all | solution.py:84
  17.3 2.9 %copy.38 = bf16[1,1024,1024]{1,2,0:T(8,128)(2,1)S(1)} copy(bf16[1,1024,1024]{2,1,0:T(8,128)(2,1)} %param.4) | data formatting | bytes 4194304 | tf_op args[0]
  20.2 0.0 copy-start.1
  20.2 0.1 slice_bitcast_fusion.2
  20.3 1.6 copy.44
  21.9 0.0 copy-done.1
  21.9 14.8 %all-to-all-done.1 = bf16[1,1024,4,128]{3,2,0,1:T(4,128)(2,1)} async-done(((bf16[1,1024,4,128]{3,2,0,1:T(4,128)(2,1)}), bf16[1,1024,4,128]{3,2,0,1:T(4,128)(2,1)}, u32[]{:S(2)}, u32[]{:S(2)}) %all-to-all-start.1) | async-done | bytes 1048608 | tf_op jit(solution)/shard_map/all_to_all | solution.py:84
  36.7 5.2 %all-to-all-start = ((bf16[1,1024,4,128]{3,2,0,1:T(4,128)(2,1)}), bf16[1,1024,4,128]{3,2,0,1:T(4,128)(2,1)}, u32[]{:S(2)}, u32[]{:S(2)}) async-start(bf16[1,1024,4,128]{3,2,0,1:T(4,128)(2,1)} %copy.44), calls=%async_computation | async-start | bytes 2097152 | tf_op jit(solution)/shard_map/all_to_all | solution.py:83
  41.9 2.9 %copy.42 = bf16[1,1024,1024]{1,2,0:T(8,128)(2,1)S(1)} copy(bf16[1,1024,1024]{2,1,0:T(8,128)(2,1)} %param.6) | data formatting | bytes 4194304 | tf_op args[2]
  44.7 0.1 slice_bitcast_fusion
  44.8 1.5 copy.50
  46.3 1.3 iota_compare_fusion
  47.6 13.7 %all-to-all-done = bf16[1,1024,4,128]{3,2,0,1:T(4,128)(2,1)} async-done(((bf16[1,1024,4,128]{3,2,0,1:T(4,128)(2,1)}), bf16[1,1024,4,128]{3,2,0,1:T(4,128)(2,1)}, u32[]{:S(2)}, u32[]{:S(2)}) %all-to-all-start) | async-done | bytes 1048608 | tf_op jit(solution)/shard_map/all_to_all | solution.py:83
  61.4 4.7 %all-to-all-start.2 = ((bf16[1,1024,4,128]{3,2,0,1:T(4,128)(2,1)}), bf16[1,1024,4,128]{3,2,0,1:T(4,128)(2,1)S(1)}, u32[]{:S(2)}, u32[]{:S(2)}) async-start(bf16[1,1024,4,128]{3,2,0,1:T(4,128)(2,1)} %copy.50), calls=%async_computation.2 | async-start | bytes 2097152 | tf_op jit(solution)/shard_map/all_to_all | solution.py:85
  66.0 11.7 %fusion.43 = (f32[4,1024]{1,0:T(4,128)S(1)}, f32[4,1024,1024]{1,2,0:T(8,128)}) fusion(pred[1024,1024]{0,1:T(8,128)(4,1)} %iota_compare_fusion, bf16[1,1024,1,2,4,128]{1,5,4,3,2,0:T(8,128)(2,1)} %bitcast.59, bf16[1,1024,1,2,4,128]{1,5,4,3,2,0:T(8,128)(2,1)} %bitcast.57), kind=kOutput, calls=%fused_computation.43 | convolution fusion | flops 1090520064 | bytes 19939328 | tf_op jit(solution)/shard_map/while/body/eval_jaxpr/sub | solution.py:30
  77.8 4.8 %fusion.38 = (f32[16,4,64]{2,1,0:T(4,128)S(1)}, f32[16,4,64,64]{2,3,1,0:T(8,128)}) fusion(pred[64,64]{0,1:T(8,128)(4,1)S(1)} %iota_compare_fusion.1, bf16[64,16,4,128]{3,2,1,0:T(4,128)(2,1)} %bitcast.11, bf16[64,16,4,128]{3,2,1,0:T(4,128)(2,1)} %bitcast.9), kind=kOutput, calls=%fused_computation.42 | convolution fusion | flops 68157504 | bytes 3166208 | tf_op jit(solution)/shard_map/sub | solution.py:30
  82.6 2.9 %all-to-all-done.2 = bf16[1,1024,4,128]{3,2,0,1:T(4,128)(2,1)S(1)} async-done(((bf16[1,1024,4,128]{3,2,0,1:T(4,128)(2,1)}), bf16[1,1024,4,128]{3,2,0,1:T(4,128)(2,1)S(1)}, u32[]{:S(2)}, u32[]{:S(2)}) %all-to-all-start.2) | async-done | bytes 1048608 | tf_op jit(solution)/shard_map/all_to_all | solution.py:85
  85.5 2.9 %fusion.11 = bf16[64,16,4,128]{3,0,2,1:T(8,128)(2,1)S(1)} fusion(f32[16,4,64,64]{2,3,1,0:T(8,128)} %get-tuple-element.16, bf16[64,16,4,128]{3,2,1,0:T(4,128)(2,1)S(1)} %bitcast.62, f32[16,4,64]{2,1,0:T(4,128)S(1)} %get-tuple-element.15), kind=kOutput, calls=%fused_computation.20 | convolution fusion | flops 68157440 | bytes 3162112 | tf_op jit(solution)/shard_map/chrs,schd->rchd/dot_general | solution.py:69
  88.4 1.8 copy.54
  90.2 7.4 %all-to-all-start.3 = ((bf16[64,16,4,128]{3,2,1,0:T(4,128)(2,1)}), bf16[64,16,4,128]{3,2,1,0:T(4,128)(2,1)S(1)}, u32[]{:S(2)}, u32[]{:S(2)}) async-start(bf16[64,16,4,128]{3,2,1,0:T(4,128)(2,1)} %copy.54), calls=%async_computation.3 | async-start | bytes 2097152 | tf_op jit(solution)/shard_map/all_to_all | solution.py:72
  97.6 8.1 %fusion.12 = bf16[1,1024,1,1,4,128]{1,5,4,3,2,0:T(8,128)(2,1)} fusion(f32[4,1024,1024]{1,2,0:T(8,128)} %get-tuple-element.24, f32[4,1024]{1,0:T(4,128)S(1)} %get-tuple-element.17, bf16[1,1024,1,2,4,128]{1,5,4,3,2,0:T(8,128)(2,1)S(1)} %bitcast.55), kind=kOutput, calls=%fused_computation.21 | convolution fusion | flops 1082654720 | bytes 18890752 | tf_op jit(solution)/shard_map/while/body/eval_jaxpr/hqk,khd->qhd/dot_general | solution.py:50
  105.7 0.0 copy-start.2
  105.7 11.4 %all-to-all-done.3 = bf16[64,16,4,128]{3,2,1,0:T(4,128)(2,1)S(1)} async-done(((bf16[64,16,4,128]{3,2,1,0:T(4,128)(2,1)}), bf16[64,16,4,128]{3,2,1,0:T(4,128)(2,1)S(1)}, u32[]{:S(2)}, u32[]{:S(2)}) %all-to-all-start.3) | async-done | bytes 1048608 | tf_op jit(solution)/shard_map/all_to_all | solution.py:72
  117.1 0.7 copy.56
  117.7 0.0 copy-done.2
  117.7 0.2 pad_maximum_fusion
  117.9 11.4 %convolution_convert_fusion = bf16[1024,4096]{1,0:T(8,128)(2,1)S(1)} fusion(bf16[1024,1024]{0,1:T(8,128)(2,1)S(1)} %bitcast.61, bf16[1024,4096]{1,0:T(8,128)(2,1)} %param.7), kind=kOutput, calls=%fused_computation.10 | convolution fusion | flops 8594128896 | bytes 18874368 | tf_op jit(solution)/shard_map/dot_general | solution.py:95
  129.3 96.4 %all_to_all.50 = bf16[2,1,512,4096]{3,2,1,0:T(8,128)(2,1)} all-to-all(bf16[2,1,512,4096]{3,2,1,0:T(8,128)(2,1)S(1)} %bitcast.53), channel_id=1, replica_groups=mesh['ctx'=64,'head'=2] {'head'}, dimensions={0} | all-to-all | bytes 16777216 | tf_op jit(solution)/shard_map/all_to_all | solution.py:18
  225.7 8.6 %reduce_sum.35 = bf16[512,4096]{1,0:T(8,128)(2,1)} reduce(bf16[2,1,512,4096]{3,2,1,0:T(8,128)(2,1)} %all_to_all.50, bf16[]{:T(256)} %constant.29.clone.1), dimensions={0,1}, to_apply=%region_4.5 | reduce | flops 2097152 | bytes 12582914 | tf_op jit(solution)/shard_map/reduce_sum | solution.py:19
  (1 shorter events, 0.0 us)
Async XLA Ops:
  2.9 1.8 copy-start
  4.7 32.0 %all-to-all-start.1 = ((bf16[1,1024,4,128]{3,2,0,1:T(4,128)(2,1)}), bf16[1,1024,4,128]{3,2,0,1:T(4,128)(2,1)}, u32[]{:S(2)}, u32[]{:S(2)}) async-start(bf16[1,1024,4,128]{3,2,0,1:T(4,128)(2,1)} %copy.46), calls=%async_computation.1 | async-start | bytes 2097152 | tf_op jit(solution)/shard_map/all_to_all | solution.py:84
  20.2 1.7 copy-start.1
  36.7 24.7 %all-to-all-start = ((bf16[1,1024,4,128]{3,2,0,1:T(4,128)(2,1)}), bf16[1,1024,4,128]{3,2,0,1:T(4,128)(2,1)}, u32[]{:S(2)}, u32[]{:S(2)}) async-start(bf16[1,1024,4,128]{3,2,0,1:T(4,128)(2,1)} %copy.44), calls=%async_computation | async-start | bytes 2097152 | tf_op jit(solution)/shard_map/all_to_all | solution.py:83
  61.4 24.1 %all-to-all-start.2 = ((bf16[1,1024,4,128]{3,2,0,1:T(4,128)(2,1)}), bf16[1,1024,4,128]{3,2,0,1:T(4,128)(2,1)S(1)}, u32[]{:S(2)}, u32[]{:S(2)}) async-start(bf16[1,1024,4,128]{3,2,0,1:T(4,128)(2,1)} %copy.50), calls=%async_computation.2 | async-start | bytes 2097152 | tf_op jit(solution)/shard_map/all_to_all | solution.py:85
  90.2 26.9 %all-to-all-start.3 = ((bf16[64,16,4,128]{3,2,1,0:T(4,128)(2,1)}), bf16[64,16,4,128]{3,2,1,0:T(4,128)(2,1)S(1)}, u32[]{:S(2)}, u32[]{:S(2)}) async-start(bf16[64,16,4,128]{3,2,1,0:T(4,128)(2,1)} %copy.54), calls=%async_computation.3 | async-start | bytes 2097152 | tf_op jit(solution)/shard_map/all_to_all | solution.py:72
  105.7 12.1 %copy-start.2 = (bf16[1,1024,1,1,4,128]{1,5,4,3,2,0:T(8,128)(2,1)S(1)}, bf16[1,1024,1,1,4,128]{1,5,4,3,2,0:T(8,128)(2,1)}, u32[]{:S(2)}) copy-start(bf16[1,1024,1,1,4,128]{1,5,4,3,2,0:T(8,128)(2,1)} %fusion.12) | copy-start | bytes 3145732
where the time goes:
time: 235 us; the launch traced here: 234 us
  blocking collectives  96.4 us (41%)
  waiting for transfers between devices  42.8 us (18%)
  matrix products  38.9 us (17%)
  starting transfers between devices  30 us (13%)
  local copies, waits for them, and re-layouts  16 us (7%)
  other arithmetic  10.2 us (4%)
    all_to_all x1, blocking collectives, summed_on_arrival(): parts = lax.all_to_all(in_blocks(x, dim, devices), axis, 0, 0, tiled=True)  96.4 us
    sub x2, matrix products, normalized(): expo = jnp.exp(scores - top)  16.5 us
    all_to_all x1, waiting for transfers between devices, on_device(): lax.all_to_all(col_triple[1], 'ctx', split_axis=1, concat_axis=0, tiled=T...  14.8 us
    all_to_all x1, waiting for transfers between devices, on_device(): lax.all_to_all(col_triple[0], 'ctx', split_axis=1, concat_axis=0, tiled=T...  13.7 us
    all_to_all x1, starting transfers between devices, on_device(): lax.all_to_all(col_triple[1], 'ctx', split_axis=1, concat_axis=0, tiled=T...  12.7 us
    dot_general x1, matrix products, on_device(): partial_value = jnp.dot(joined, w_out, preferred_element_type=jnp.float32)  11.4 us
    all_to_all x1, waiting for transfers between devices, column_attention(): lax.all_to_all(attended, 'ctx', split_axis=0, concat_axis=1, tiled=True)  11.4 us
    reduce_sum x1, other arithmetic, summed_on_arrival(): return jnp.sum(parts.astype(jnp.float32), axis=0)  8.63 us
  transfers between devices with their start and end apart: 4, of which 4 were waited for; matrix products, arithmetic and copies ran while one was open for 15% of the time, Pallas kernels for 0%

commit v1 on v0

--- a/solution.py
+++ b/solution.py
@@ -69,7 +69,10 @@
     attended = jnp.einsum(
         "chrs,schd->rchd", weights, values, preferred_element_type=jnp.float32
     ).astype(jnp.bfloat16)
-    return lax.all_to_all(attended, "ctx", split_axis=0, concat_axis=1, tiled=True)
+    return jnp.concatenate(
+        lax.all_to_all(jnp.stack(jnp.split(attended, lax.axis_size("ctx"), axis=0)), "ctx", 0, 0),
+        axis=1,
+    )
 
 
 def on_device(queries, keys, values, w_out):

time: 235 us -> 275 us (1.17)
  local copies, waits for them, and re-layouts: 16 us -> 55.6 us
    unnamed x9 -> x72, local copies, waits for them, and re-layouts: 8.59 us -> 47.1 us
    all_to_all x1, starting transfers between devices: 5.19 us -> 12.7 us  [on_device(): lax.all_to_all(col_triple[0], 'ctx', split_axis=1, concat_axis=0, tiled=T...]
    all_to_all x1, starting transfers between devices: 12.7 us -> 5.19 us  [on_device(): lax.all_to_all(col_triple[1], 'ctx', split_axis=1, concat_axis=0, tiled=T...]
  transfers between devices with their start and end apart: 4 -> 4, of which waited for: 4 -> 4; matrix products, arithmetic and copies ran while one was open for 15% -> 13% of each run, Pallas kernels for 0% -> 0%
where the time goes in v1:
time: 275 us; the launch traced here: 274 us
  blocking collectives  96.4 us (35%)
  local copies, waits for them, and re-layouts  55.6 us (20%)
  waiting for transfers between devices  42.8 us (16%)
  matrix products  38.9 us (14%)
  starting transfers between devices  30 us (11%)
  other arithmetic  10.2 us (4%)
    all_to_all x1, blocking collectives, summed_on_arrival(): parts = lax.all_to_all(in_blocks(x, dim, devices), axis, 0, 0, tiled=True)  96.4 us
    unnamed x72, local copies, waits for them, and re-layouts  47.1 us
    sub x2, matrix products, normalized(): expo = jnp.exp(scores - top)  16.6 us
    all_to_all x1, waiting for transfers between devices, on_device(): lax.all_to_all(col_triple[0], 'ctx', split_axis=1, concat_axis=0, tiled=T...  14.8 us
    all_to_all x1, waiting for transfers between devices, on_device(): lax.all_to_all(col_triple[1], 'ctx', split_axis=1, concat_axis=0, tiled=T...  13.7 us
    all_to_all x1, starting transfers between devices, on_device(): lax.all_to_all(col_triple[0], 'ctx', split_axis=1, concat_axis=0, tiled=T...  12.7 us
    dot_general x1, matrix products, on_device(): partial_value = jnp.dot(joined, w_out, preferred_element_type=jnp.float32)  11.4 us
    all_to_all x1, waiting for transfers between devices, column_attention(): lax.all_to_all(jnp.stack(jnp.split(attended, lax.axis_size('ctx'), axis=0...  11.4 us
  transfers between devices with their start and end apart: 4, of which 4 were waited for; matrix products, arithmetic and copies ran while one was open for 13% of the time, Pallas kernels for 0%

profile of v1, /device:TPU:1, one launch (start us, length us, event | category | flops | bytes accessed | tf_op | source)
XLA Modules:
  0.0 274.2 jit_solution(10978007434938377049)
XLA Ops:
  0.0 2.9 %copy.2953 = bf16[1,1024,1024]{1,2,0:T(8,128)(2,1)S(1)} copy(bf16[1,1024,1024]{2,1,0:T(8,128)(2,1)} %param.4) | data formatting | bytes 4194304 | tf_op args[0]
  3.0 1.6 copy.2959
  4.6 12.7 %all-to-all-start = ((bf16[1,1024,4,128]{3,2,0,1:T(4,128)(2,1)}), bf16[1,1024,4,128]{3,2,0,1:T(4,128)(2,1)}, u32[]{:S(2)}, u32[]{:S(2)}) async-start(bf16[1,1024,4,128]{3,2,0,1:T(4,128)(2,1)} %copy.2959), calls=%async_computation | async-start | bytes 2097152 | tf_op jit(solution)/shard_map/all_to_all | solution.py:86
  17.2 2.9 %copy.2955 = bf16[1,1024,1024]{1,2,0:T(8,128)(2,1)S(1)} copy(bf16[1,1024,1024]{2,1,0:T(8,128)(2,1)} %param.5) | data formatting | bytes 4194304 | tf_op args[1]
  20.2 1.6 copy.2961
  21.8 14.8 %all-to-all-done = bf16[1,1024,4,128]{3,2,0,1:T(4,128)(2,1)} async-done(((bf16[1,1024,4,128]{3,2,0,1:T(4,128)(2,1)}), bf16[1,1024,4,128]{3,2,0,1:T(4,128)(2,1)}, u32[]{:S(2)}, u32[]{:S(2)}) %all-to-all-start) | async-done | bytes 1048608 | tf_op jit(solution)/shard_map/all_to_all | solution.py:86
  36.6 5.2 %all-to-all-start.1 = ((bf16[1,1024,4,128]{3,2,0,1:T(4,128)(2,1)}), bf16[1,1024,4,128]{3,2,0,1:T(4,128)(2,1)}, u32[]{:S(2)}, u32[]{:S(2)}) async-start(bf16[1,1024,4,128]{3,2,0,1:T(4,128)(2,1)} %copy.2961), calls=%async_computation.1 | async-start | bytes 2097152 | tf_op jit(solution)/shard_map/all_to_all | solution.py:87
  41.8 2.9 %copy.2957 = bf16[1,1024,1024]{1,2,0:T(8,128)(2,1)S(1)} copy(bf16[1,1024,1024]{2,1,0:T(8,128)(2,1)} %param.6) | data formatting | bytes 4194304 | tf_op args[2]
  44.7 1.5 copy.2965
  46.2 1.3 iota_compare_fusion
  47.5 13.7 %all-to-all-done.1 = bf16[1,1024,4,128]{3,2,0,1:T(4,128)(2,1)} async-done(((bf16[1,1024,4,128]{3,2,0,1:T(4,128)(2,1)}), bf16[1,1024,4,128]{3,2,0,1:T(4,128)(2,1)}, u32[]{:S(2)}, u32[]{:S(2)}) %all-to-all-start.1) | async-done | bytes 1048608 | tf_op jit(solution)/shard_map/all_to_all | solution.py:87
  61.3 4.7 %all-to-all-start.2 = ((bf16[1,1024,4,128]{3,2,0,1:T(4,128)(2,1)}), bf16[1,1024,4,128]{3,2,0,1:T(4,128)(2,1)S(1)}, u32[]{:S(2)}, u32[]{:S(2)}) async-start(bf16[1,1024,4,128]{3,2,0,1:T(4,128)(2,1)} %copy.2965), calls=%async_computation.2 | async-start | bytes 2097152 | tf_op jit(solution)/shard_map/all_to_all | solution.py:88
  66.0 11.8 %fusion.47 = (f32[4,1024]{1,0:T(4,128)S(1)}, f32[4,1024,1024]{1,2,0:T(8,128)}) fusion(pred[1024,1024]{0,1:T(8,128)(4,1)} %iota_compare_fusion, bf16[1,1024,1,2,4,128]{1,5,4,3,2,0:T(8,128)(2,1)} %bitcast.186, bf16[1,1024,1,2,4,128]{1,5,4,3,2,0:T(8,128)(2,1)} %bitcast.188), kind=kOutput, calls=%fused_computation.142 | convolution fusion | flops 1090520064 | bytes 19939328 | tf_op jit(solution)/shard_map/while/body/eval_jaxpr/sub | solution.py:30
  77.7 4.8 %fusion.42 = (f32[16,4,64]{2,1,0:T(4,128)S(1)}, f32[16,4,64,64]{2,3,1,0:T(8,128)}) fusion(pred[64,64]{0,1:T(8,128)(4,1)S(1)} %iota_compare_fusion.1, bf16[64,16,4,128]{3,2,1,0:T(4,128)(2,1)} %bitcast.11, bf16[64,16,4,128]{3,2,1,0:T(4,128)(2,1)} %bitcast.9), kind=kOutput, calls=%fused_computation.141 | convolution fusion | flops 68157504 | bytes 3166208 | tf_op jit(solution)/shard_map/sub | solution.py:30
  82.5 2.9 %all-to-all-done.2 = bf16[1,1024,4,128]{3,2,0,1:T(4,128)(2,1)S(1)} async-done(((bf16[1,1024,4,128]{3,2,0,1:T(4,128)(2,1)}), bf16[1,1024,4,128]{3,2,0,1:T(4,128)(2,1)S(1)}, u32[]{:S(2)}, u32[]{:S(2)}) %all-to-all-start.2) | async-done | bytes 1048608 | tf_op jit(solution)/shard_map/all_to_all | solution.py:88
  85.4 2.9 %fusion.11 = bf16[64,16,4,128]{3,0,2,1:T(8,128)(2,1)S(1)} fusion(f32[16,4,64,64]{2,3,1,0:T(8,128)} %get-tuple-element.88, bf16[64,16,4,128]{3,2,1,0:T(4,128)(2,1)S(1)} %bitcast.191, f32[16,4,64]{2,1,0:T(4,128)S(1)} %get-tuple-element.87), kind=kOutput, calls=%fused_computation.20 | convolution fusion | flops 68157440 | bytes 3162112 | tf_op jit(solution)/shard_map/chrs,schd->rchd/dot_general | solution.py:69
  88.5 0.7 fusion.40
  89.1 0.7 fusion.38
  89.8 0.7 fusion.39
  90.5 0.6 constant_dynamic-update-slice_fusion.63
  91.3 0.6 constant_dynamic-update-slice_fusion.62
  92.0 0.6 constant_dynamic-update-slice_fusion.61
  92.6 0.6 constant_dynamic-update-slice_fusion.60
  93.2 0.6 constant_dynamic-update-slice_fusion.59
  93.8 0.6 constant_dynamic-update-slice_fusion.58
  94.4 0.6 constant_dynamic-update-slice_fusion.57
  95.0 0.6 constant_dynamic-update-slice_fusion.56
  95.6 0.6 constant_dynamic-update-slice_fusion.55
  96.2 0.6 constant_dynamic-update-slice_fusion.54
  96.9 0.6 constant_dynamic-update-slice_fusion.53
  97.5 0.6 constant_dynamic-update-slice_fusion.52
  98.1 0.6 constant_dynamic-update-slice_fusion.51
  98.7 0.6 constant_dynamic-update-slice_fusion.50
  99.3 0.6 constant_dynamic-update-slice_fusion.49
  99.9 0.6 constant_dynamic-update-slice_fusion.48
  100.5 0.6 constant_dynamic-update-slice_fusion.47
  101.1 0.6 constant_dynamic-update-slice_fusion.46
  101.8 0.6 constant_dynamic-update-slice_fusion.45
  102.4 0.6 constant_dynamic-update-slice_fusion.44
  103.6 0.6 constant_dynamic-update-slice_fusion.42
  104.2 0.6 constant_dynamic-update-slice_fusion.41
  129.9 7.5 %all-to-all-start.3 = ((bf16[64,1,16,4,128]{4,3,2,1,0:T(4,128)(2,1)}), bf16[64,1,16,4,128]{4,3,2,1,0:T(4,128)(2,1)S(1)}, u32[]{:S(2)}, u32[]{:S(2)}) async-start(bf16[64,1,16,4,128]{4,3,2,1,0:T(4,128)(2,1)} %constant_dynamic-update-slice_fusion), calls=%async_computation.3 | async-start | bytes 2097152 | tf_op jit(solution)/shard_map/all_to_all | solution.py:73
  137.4 8.1 %fusion.12 = bf16[1,1024,1,1,4,128]{1,5,4,3,2,0:T(8,128)(2,1)} fusion(f32[4,1024,1024]{1,2,0:T(8,128)} %get-tuple-element.90, f32[4,1024]{1,0:T(4,128)S(1)} %get-tuple-element.89, bf16[1,1024,1,2,4,128]{1,5,4,3,2,0:T(8,128)(2,1)S(1)} %bitcast.184), kind=kOutput, calls=%fused_computation.21 | convolution fusion | flops 1082654720 | bytes 18890752 | tf_op jit(solution)/shard_map/while/body/eval_jaxpr/hqk,khd->qhd/dot_general | solution.py:50
  145.4 11.4 %all-to-all-done.3 = bf16[64,1,16,4,128]{4,3,2,1,0:T(4,128)(2,1)S(1)} async-done(((bf16[64,1,16,4,128]{4,3,2,1,0:T(4,128)(2,1)}), bf16[64,1,16,4,128]{4,3,2,1,0:T(4,128)(2,1)S(1)}, u32[]{:S(2)}, u32[]{:S(2)}) %all-to-all-start.3) | async-done | bytes 1048608 | tf_op jit(solution)/shard_map/all_to_all | solution.py:73
  156.8 0.7 copy.3032
  157.7 11.4 %convolution_convert_fusion = bf16[1024,4096]{1,0:T(8,128)(2,1)S(1)} fusion(bf16[1024,1024]{0,1:T(8,128)(2,1)S(1)} %bitcast.190, bf16[1024,4096]{1,0:T(8,128)(2,1)} %param.7), kind=kOutput, calls=%fused_computation.10 | convolution fusion | flops 8594128896 | bytes 18874368 | tf_op jit(solution)/shard_map/dot_general | solution.py:98
  169.1 96.4 %all_to_all.46 = bf16[2,1,512,4096]{3,2,1,0:T(8,128)(2,1)} all-to-all(bf16[2,1,512,4096]{3,2,1,0:T(8,128)(2,1)S(1)} %bitcast.182), channel_id=1, replica_groups=mesh['ctx'=64,'head'=2] {'head'}, dimensions={0} | all-to-all | bytes 16777216 | tf_op jit(solution)/shard_map/all_to_all | solution.py:18
  265.6 8.6 %reduce_sum.35 = bf16[512,4096]{1,0:T(8,128)(2,1)} reduce(bf16[2,1,512,4096]{3,2,1,0:T(8,128)(2,1)} %all_to_all.46, bf16[]{:T(256)} %constant.29.clone.1), dimensions={0,1}, to_apply=%region_4.5 | reduce | flops 2097152 | bytes 12582914 | tf_op jit(solution)/shard_map/reduce_sum | solution.py:19
  (70 shorter events, 26.4 us)
Async XLA Ops:
  2.9 1.7 copy-start
  4.6 32.0 %all-to-all-start = ((bf16[1,1024,4,128]{3,2,0,1:T(4,128)(2,1)}), bf16[1,1024,4,128]{3,2,0,1:T(4,128)(2,1)}, u32[]{:S(2)}, u32[]{:S(2)}) async-start(bf16[1,1024,4,128]{3,2,0,1:T(4,128)(2,1)} %copy.2959), calls=%async_computation | async-start | bytes 2097152 | tf_op jit(solution)/shard_map/all_to_all | solution.py:86
  20.1 1.7 copy-start.1
  36.6 24.7 %all-to-all-start.1 = ((bf16[1,1024,4,128]{3,2,0,1:T(4,128)(2,1)}), bf16[1,1024,4,128]{3,2,0,1:T(4,128)(2,1)}, u32[]{:S(2)}, u32[]{:S(2)}) async-start(bf16[1,1024,4,128]{3,2,0,1:T(4,128)(2,1)} %copy.2961), calls=%async_computation.1 | async-start | bytes 2097152 | tf_op jit(solution)/shard_map/all_to_all | solution.py:87
  61.3 24.1 %all-to-all-start.2 = ((bf16[1,1024,4,128]{3,2,0,1:T(4,128)(2,1)}), bf16[1,1024,4,128]{3,2,0,1:T(4,128)(2,1)S(1)}, u32[]{:S(2)}, u32[]{:S(2)}) async-start(bf16[1,1024,4,128]{3,2,0,1:T(4,128)(2,1)} %copy.2965), calls=%async_computation.2 | async-start | bytes 2097152 | tf_op jit(solution)/shard_map/all_to_all | solution.py:88
  129.9 26.9 %all-to-all-start.3 = ((bf16[64,1,16,4,128]{4,3,2,1,0:T(4,128)(2,1)}), bf16[64,1,16,4,128]{4,3,2,1,0:T(4,128)(2,1)S(1)}, u32[]{:S(2)}, u32[]{:S(2)}) async-start(bf16[64,1,16,4,128]{4,3,2,1,0:T(4,128)(2,1)} %constant_dynamic-update-slice_fusion), calls=%async_computation.3 | async-start | bytes 2097152 | tf_op jit(solution)/shard_map/all_to_all | solution.py:73
  145.4 12.1 %copy-start.2 = (bf16[1,1024,1,1,4,128]{1,5,4,3,2,0:T(8,128)(2,1)S(1)}, bf16[1,1024,1,1,4,128]{1,5,4,3,2,0:T(8,128)(2,1)}, u32[]{:S(2)}) copy-start(bf16[1,1024,1,1,4,128]{1,5,4,3,2,0:T(8,128)(2,1)} %fusion.12) | copy-start | bytes 3145732
